TPU v7x, 128 devices: a whole 4x4x4 slice. The times are simulated.
128 devices in a mesh: seg: 8 (over x, core), row: 16 (over z, y).
Axes of the slice: x: 4, y: 4, z: 4, core: 2. Of those that a mesh axis runs over, the one named last changes fastest.
Arguments:
- wavefunction: bfloat16 [8192, 4, 1024], P(('seg', 'row')), may hold values from -110 to 110
- left_block: bfloat16 [8192, 1024], P(('seg', 'row')), may hold values from -2 to 2, as said below
- left_edge: bfloat16 [8192, 1024], P(('seg', 'row')), may hold values from -2 to 2, as said below
- right_block: bfloat16 [8192, 1024], P('seg'), may hold values from -2 to 2, as said below
- right_edge: bfloat16 [8192, 1024], P('seg'), may hold values from -2 to 2, as said below
- fields: float32 [8, 2], P('seg'), may hold values from 0.3 to 3
- bond_values: float32 [8, 1024], P('seg'), may hold values from 0.5 to 2
- kept_rank: int32 [8], P('seg'), may hold values from 512 to 1024
Outputs:
- updated_wave: bfloat16 [8192, 4, 1024], P(('seg', 'row'))
- joined_wave: bfloat16 [8192, 4, 1024], P(('seg', 'row'))
- energies: float32 [8], P('seg')
Inputs may be any that keep to these rules, and one draw needn't show every extreme that they name: `left_block`: each segment's 1024 x 1024 block is symmetric. `left_edge`: each segment's 1024 x 1024 block is symmetric. `right_block`: each segment's 1024 x 1024 block is symmetric. `right_edge`: each segment's 1024 x 1024 block is symmetric.
All inputs are finite; a program needn't handle non-finite values.
Results may differ from a plain program's by a relative error of at most 0.006.
Values may be sent and summed in bfloat16 or wider, within the bound.
No kernel may reach another device: no remote copies, remote signals or barrier semaphores. Data moves between devices by JAX's collectives and lax.ppermute only.
A program may use at most 64 MiB of HBM per device.

v0:
```python
import jax
import jax.numpy as jnp
from jax import lax
from jax.sharding import PartitionSpec as P

STEP_SIZE = 0.25


def copy_for_each(value, axis):
    copies = jnp.broadcast_to(value, (lax.axis_size(axis), *value.shape))
    return lax.all_to_all(copies, axis, split_axis=0, concat_axis=0, tiled=True)


def over_copies(value, axis):
    everything = copy_for_each(value, axis)
    return jnp.sum(everything, axis=0)


def in_one(arrays, axis):
    ends = [0]
    for a in arrays:
        ends.append(ends[-1] + a.size)
    running = over_copies(jnp.concatenate([a.ravel() for a in arrays]), axis)
    return tuple((running[b:e].reshape(a.shape) for a, b, e in zip(arrays, ends, ends[1:])))


def split_up(value, dim, count):
    before, after = (value.shape[:dim], value.shape[dim + 1 :])
    return jnp.moveaxis(value.reshape(*before, count, -1, *after), dim, 0)


def sent_and_summed(value, axis, dim):
    parts = split_up(value, dim, lax.axis_size(axis))
    arrived = lax.all_to_all(parts, axis, split_axis=0, concat_axis=0, tiled=True)
    return arrived.sum(axis=0)


def passed_along(value, axis, steps):
    count = lax.axis_size(axis)
    first, last = (max(0, -steps), min(count, count - steps))
    return lax.ppermute(value, axis, [(source, source + steps) for source in range(first, last)])


def row_total(summands):
    return in_one((summands[0], summands[1], summands[2]), "row")


def body(
    wavefunction, left_block, left_edge, right_block, right_edge, fields, bond_values, kept_rank
):
    row_count = wavefunction.shape[0]
    bond_dim = wavefunction.shape[2]
    shard_rows = lax.all_gather(wavefunction, "row", axis=0, tiled=True)
    how_many = shard_rows.shape[0]
    rows_flat = shard_rows.reshape(how_many, 4 * bond_dim)
    left_h = jnp.dot(left_block, rows_flat, preferred_element_type=jnp.float32)
    left_z = jnp.dot(left_edge, rows_flat, preferred_element_type=jnp.float32)
    left_h = left_h.reshape(row_count, 4, bond_dim)
    left_z = left_z.reshape(row_count, 4, bond_dim)
    columns = wavefunction.reshape(row_count * 4, bond_dim)
    right_h = jnp.dot(columns, right_block, preferred_element_type=jnp.float32).reshape(
        row_count, 4, bond_dim
    )
    right_z = jnp.dot(columns, right_edge, preferred_element_type=jnp.float32).reshape(
        row_count, 4, bond_dim
    )
    sign_one = jnp.array([1.0, 1.0, -1.0, -1.0], jnp.float32).reshape(1, 4, 1)
    sign_two = jnp.array([1.0, -1.0, 1.0, -1.0], jnp.float32).reshape(1, 4, 1)
    values = wavefunction.astype(jnp.float32)
    swap_one = jnp.concatenate([values[:, 2:4], values[:, 0:2]], 1)
    swap_two = jnp.stack([values[:, 1], values[:, 0], values[:, 3], values[:, 2]], 1)
    field_pair = fields[0]
    applied = (
        left_h
        + sign_one * left_z
        + right_h
        + sign_two * right_z
        - sign_one * sign_two * values
        - field_pair[0] * swap_one
        - field_pair[1] * swap_two
    )
    squares_local = jnp.sum(values * values)
    rayleigh_local = jnp.sum(values * applied)
    squares, rayleigh, image_square = row_total(
        (squares_local, rayleigh_local, jnp.sum(applied * applied))
    )
    energy = rayleigh / squares
    stepped = values - STEP_SIZE * (applied - energy * values)
    renorm = squares + STEP_SIZE * STEP_SIZE * (image_square - rayleigh * rayleigh / squares)
    wave_new = (stepped * jnp.sqrt(bond_dim / renorm)).astype(jnp.bfloat16)
    new_columns = wave_new.reshape(row_count * 4, bond_dim)
    gram = sent_and_summed(
        lax.dot_general(
            new_columns, new_columns, (((0,), (0,)), ((), ())), preferred_element_type=jnp.float32
        ),
        "row",
        0,
    )
    offset = lax.axis_index("row") * row_count
    positions = jnp.arange(bond_dim)
    inverse = jnp.where(positions < kept_rank[0], 1.0 / bond_values[0], 0.0)
    inverse_rows = lax.dynamic_slice_in_dim(inverse, offset, row_count, 0)
    weighted = (inverse_rows[:, None] * gram * inverse[None, :]).astype(jnp.bfloat16)
    previous = passed_along(weighted, "seg", 1)
    shard_rows = lax.all_gather(wave_new, "row", axis=0, tiled=True)
    how_many = shard_rows.shape[0]
    joined = jnp.dot(
        previous, shard_rows.reshape(how_many, 4 * bond_dim), preferred_element_type=jnp.float32
    )
    joined_wave = joined.astype(jnp.bfloat16).reshape(row_count, 4, bond_dim)
    return (wave_new, joined_wave, energy.reshape(1))


def solution(mesh):
    in_specs = (
        P(("seg", "row"), None, None),
        P(("seg", "row"), None),
        P(("seg", "row"), None),
        P("seg", None),
        P("seg", None),
        P("seg", None),
        P("seg", None),
        P("seg"),
    )
    out_specs = (P(("seg", "row"), None, None), P(("seg", "row"), None, None), P("seg"))
    return jax.shard_map(body, mesh=mesh, in_specs=in_specs, out_specs=out_specs, check_vma=False)
```

profile of v0, /device:TPU:1, one launch (start us, length us, event | category | flops | bytes accessed | tf_op | source)
XLA Modules:
  0.0 274.9 jit_solution(6586143170617328613)
XLA Ops:
  7.2 0.0 copy-start
  7.2 0.0 all-gather.3.cloned.1.call-start
  7.2 0.7 all-gather.3.cloned.1.call-update
  7.9 0.0 all-gather.5.cloned.1.call-start
  8.0 1.3 fusion.46
  9.3 1.2 copy_convert_fusion
  10.5 0.9 fusion.43
  11.4 0.9 fusion.44
  12.3 3.4 %fusion.20 = f32[64,4,1024]{2,0,1:T(8,128)} fusion(bf16[1024,1024]{1,0:T(8,128)(2,1)} %param.14, f32[4]{0:T(128)} %constant.25.clone, bf16[64,4,1024]{2,1,0:T(4,128)(2,1)} %param.10), kind=kOutput, calls=%fused_computation.13 | convolution fusion | flops 537133056 | bytes 3670032 | tf_op jit(solution)/shard_map/dot_general | solution.py:64
  15.7 68.5 %all-gather.3.cloned.1.call-done = bf16[1024,4,1024]{2,1,0:T(4,128)(2,1)} async-done(((bf16[64,4,1024]{2,1,0:T(4,128)(2,1)}), bf16[1024,4,1024]{2,1,0:T(4,128)(2,1)}) %all-gather.3.cloned.1.call-update) | async-done | bytes 8388624 | tf_op jit(solution)/shard_map/all_gather | solution.py:53
  84.1 13.7 %copy.60 = bf16[1024,4,1024]{0,2,1:T(8,128)(2,1)} copy(bf16[1024,4,1024]{2,1,0:T(4,128)(2,1)} %all-gather.3.cloned.1.call-done) | data formatting | bytes 16777216 | tf_op jit(solution)/shard_map/reshape | solution.py:55
  97.8 0.0 copy-done.9
  97.9 0.0 copy-start.2
  97.9 0.0 copy-start.5
  97.9 0.0 copy-start.6
  97.9 0.0 copy-start.12
  97.9 6.2 %fusion.29 = f32[64,4,1024]{2,0,1:T(8,128)S(1)} fusion(bf16[1024,4,1024]{0,2,1:T(8,128)(2,1)} %copy.60, f32[4]{0:T(128)S(1)} %copy-done.11, bf16[64,1024]{1,0:T(8,128)(2,1)S(1)} %copy-done.9), kind=kOutput, calls=%fused_computation.21 | convolution fusion | flops 537133056 | bytes 9568272 | tf_op jit(solution)/shard_map/dot_general | solution.py:57
  104.1 3.6 %fusion.26 = f32[64,4,1024]{2,0,1:T(8,128)S(1)} fusion(f32[64,4,1024]{2,0,1:T(8,128)S(1)} %fusion.29, bf16[1024,4,1024]{0,2,1:T(8,128)(2,1)S(1)} %copy-done.1, bf16[64,1024]{1,0:T(8,128)(2,1)} %param.11), kind=kOutput, calls=%fused_computation.20 | convolution fusion | flops 537133056 | bytes 10616832 | tf_op jit(solution)/shard_map/dot_general | solution.py:56
  107.7 0.0 copy-done
  107.7 0.0 copy-done.2
  107.7 0.0 copy-done.4
  107.7 0.0 copy-done.5
  107.7 0.0 copy-done.6
  107.7 0.0 copy-done.7
  107.8 4.0 %fusion.33 = (f32[]{:T(128)}, f32[]{:T(128)}, f32[]{:T(128)}, f32[64,4,1024]{2,0,1:T(8,128)}) fusion(bf16[64,4,1024]{2,1,0:T(4,128)(2,1)S(1)} %copy-done.2, f32[64,1,1024]{2,0,1:T(8,128)S(1)} %copy-done.8, f32[64,1,1024]{2,0,1:T(8,128)S(1)} %copy-done.6, f32[64,1,1024]{2,0,1:T(8,128)S(1)} %copy-done.7, f32[64,1,1024]{2,0,1:T(8,128)S(1)} %get-tuple-element.26, ...), kind=kOutput, calls=%fused_computation.23 | convolution fusion | flops 541851648 | bytes 7864356 | tf_op jit(solution)/shard_map/dot_general | solution.py:61
  111.8 1.9 pad_maximum_fusion
  113.8 11.2 %all_to_all.11 = f32[16,1,3]{2,1,0:T(1,128)S(1)} all-to-all(f32[16,1,3]{2,1,0:T(1,128)S(1)} %broadcast_in_dim.11), channel_id=1, replica_groups=mesh['seg'=8,'row'=16] {'row'}, dimensions={0} | all-to-all | bytes 384 | tf_op jit(solution)/shard_map/all_to_all | solution.py:11
  125.0 0.6 fusion.45
  130.3 2.3 fusion.37
  132.6 0.0 all-gather.5.cloned.1.call-update
  132.6 1.5 copy.59
  134.1 0.0 copy-start.3
  134.1 0.0 copy-start.10
  134.1 0.1 reshape.91
  134.2 1.0 reshape.83
  135.2 2.1 copy.57
  137.3 3.7 %fusion.47 = f32[16,64,1024]{2,1,0:T(8,128)} fusion(bf16[16,64,256]{2,1,0:T(8,128)(2,1)} %bitcast.61, bf16[256,1024,1]{1,0,2:T(8,128)(2,1)S(1)} %reshape.91), kind=kOutput, calls=%fused_computation.46 | convolution fusion | flops 536870912 | bytes 5242880 | tf_op jit(solution)/shard_map/dot_general | solution.py:93
  141.0 4.6 %all-to-all-start.1 = ((f32[16,64,1024]{2,1,0:T(8,128)}), f32[16,64,1024]{2,1,0:T(8,128)}, u32[]{:S(2)}, u32[]{:S(2)}) async-start(f32[16,64,1024]{2,1,0:T(8,128)} %fusion.47), calls=%async_computation.1 | async-start | bytes 8388608 | tf_op jit(solution)/shard_map/all_to_all | solution.py:34
  146.3 0.1 dynamic_slice.3
  146.4 67.0 %all-to-all-done.1 = f32[16,64,1024]{2,1,0:T(8,128)} async-done(((f32[16,64,1024]{2,1,0:T(8,128)}), f32[16,64,1024]{2,1,0:T(8,128)}, u32[]{:S(2)}, u32[]{:S(2)}) %all-to-all-start.1) | async-done | bytes 4194336 | tf_op jit(solution)/shard_map/all_to_all | solution.py:34
  213.4 2.5 reduce_sum.49
  215.9 0.1 multiply_convert_fusion
  216.0 5.8 %collective-permute-start = (bf16[64,1024]{1,0:T(8,128)(2,1)S(1)}, bf16[64,1024]{1,0:T(8,128)(2,1)S(1)}, u32[]{:S(2)}, u32[]{:S(2)}) collective-permute-start(bf16[64,1024]{1,0:T(8,128)(2,1)S(1)} %multiply_convert_fusion), channel_id=1, source_target_pairs={{0,16},{16,32},{32,48},{48,64},{64,80},{80,96},{96,112},{1,17},{17... | collective-permute-start | bytes 393224 | tf_op jit(solution)/shard_map/ppermute | solution.py:41
  221.8 26.5 %all-gather.5.cloned.1.call-done = bf16[1024,4,1024]{2,0,1:T(8,128)(2,1)} async-done(((bf16[64,4,1024]{2,0,1:T(8,128)(2,1)}), bf16[1024,4,1024]{2,0,1:T(8,128)(2,1)}) %all-gather.5.cloned.1.call-update) | async-done | bytes 8388624 | tf_op jit(solution)/shard_map/all_gather | solution.py:105
  248.3 11.4 %copy.58 = bf16[1024,4,1024]{0,2,1:T(8,128)(2,1)} copy(bf16[1024,4,1024]{2,0,1:T(8,128)(2,1)} %all-gather.5.cloned.1.call-done) | data formatting | bytes 16777216 | tf_op jit(solution)/shard_map/all_gather | solution.py:105
  259.7 0.0 collective-permute-done
  259.7 6.0 %convolution_convert_fusion = bf16[64,4096]{1,0:T(8,128)(2,1)S(1)} fusion(bf16[64,1024]{1,0:T(8,128)(2,1)S(1)} %collective-permute-done, bf16[1024,4096]{0,1:T(8,128)(2,1)} %bitcast.60), kind=kOutput, calls=%fused_computation.4 | convolution fusion | flops 537133056 | bytes 9043968 | tf_op jit(solution)/shard_map/dot_general | solution.py:107
  265.7 1.2 reshape.85
  (16 shorter events, 0.1 us)
Async XLA Ops:
  7.2 100.5 %copy-start = (bf16[1024,1024]{1,0:T(8,128)(2,1)S(1)}, bf16[1024,1024]{1,0:T(8,128)(2,1)}, u32[]{:S(2)}) copy-start(bf16[1024,1024]{1,0:T(8,128)(2,1)} %param.13) | copy-start | bytes 6291460
  7.2 77.0 %all-gather.3.cloned.1.call-start = ((), (), s32[]{:S(2)}) async-start(), calls=%async_computation.2 | async-start | bytes 8912896 | tf_op jit(solution)/shard_map/all_gather | solution.py:53
  7.9 240.4 %all-gather.5.cloned.1.call-start = ((), (), s32[]{:S(2)}) async-start(), calls=%async_computation.3 | async-start | bytes 8912896 | tf_op jit(solution)/shard_map/all_gather | solution.py:105
  15.7 82.2 %copy-start.9 = (bf16[64,1024]{1,0:T(8,128)(2,1)S(1)}, bf16[64,1024]{1,0:T(8,128)(2,1)}, u32[]{:S(2)}) copy-start(bf16[64,1024]{1,0:T(8,128)(2,1)} %param.12) | copy-start | bytes 393220
  15.7 82.2 %copy-start.11 = (f32[4]{0:T(128)S(1)}, f32[4]{0:T(128)}, u32[]{:S(2)}) copy-start(f32[4]{0:T(128)} %constant.24.clone) | copy-start | bytes 52
  97.8 6.3 %copy-start.1 = (bf16[1024,4,1024]{0,2,1:T(8,128)(2,1)S(1)}, bf16[1024,4,1024]{0,2,1:T(8,128)(2,1)}, u32[]{:S(2)}) copy-start(bf16[1024,4,1024]{0,2,1:T(8,128)(2,1)} %copy.60) | copy-start | bytes 25165828
  97.9 9.9 %copy-start.2 = (bf16[64,4,1024]{2,1,0:T(4,128)(2,1)S(1)}, bf16[64,4,1024]{2,1,0:T(4,128)(2,1)}, u32[]{:S(2)}) copy-start(bf16[64,4,1024]{2,1,0:T(4,128)(2,1)} %param.10) | copy-start | bytes 1572868
  97.9 9.8 %copy-start.4 = (f32[64,4,1024]{2,0,1:T(8,128)S(1)}, f32[64,4,1024]{2,0,1:T(8,128)}, u32[]{:S(2)}) copy-start(f32[64,4,1024]{2,0,1:T(8,128)} %fusion.20) | copy-start | bytes 3145732
  97.9 9.8 %copy-start.5 = (f32[64,2,1024]{2,0,1:T(8,128)S(1)}, f32[64,2,1024]{2,0,1:T(8,128)}, u32[]{:S(2)}) copy-start(f32[64,2,1024]{2,0,1:T(8,128)} %get-tuple-element.31) | copy-start | bytes 1572868
  97.9 9.8 %copy-start.6 = (f32[64,1,1024]{2,0,1:T(8,128)S(1)}, f32[64,1,1024]{2,0,1:T(8,128)}, u32[]{:S(2)}) copy-start(f32[64,1,1024]{2,0,1:T(8,128)} %get-tuple-element.27) | copy-start | bytes 786436
  97.9 9.8 %copy-start.7 = (f32[64,1,1024]{2,0,1:T(8,128)S(1)}, f32[64,1,1024]{2,0,1:T(8,128)}, u32[]{:S(2)}) copy-start(f32[64,1,1024]{2,0,1:T(8,128)} %get-tuple-element.28) | copy-start | bytes 786436
  97.9 9.8 %copy-start.8 = (f32[64,1,1024]{2,0,1:T(8,128)S(1)}, f32[64,1,1024]{2,0,1:T(8,128)}, u32[]{:S(2)}) copy-start(f32[64,1,1024]{2,0,1:T(8,128)} %get-tuple-element.29) | copy-start | bytes 786436
  97.9 9.8 %copy-start.12 = (f32[4]{0:T(128)S(1)}, f32[4]{0:T(128)}, u32[]{:S(2)}) copy-start(f32[4]{0:T(128)} %constant.32) | copy-start | bytes 52
  134.1 6.9 %copy-start.3 = (bf16[64,4,1024]{2,1,0:T(4,128)(2,1)}, bf16[64,4,1024]{2,1,0:T(4,128)(2,1)S(1)}, u32[]{:S(2)}) copy-start(bf16[64,4,1024]{2,1,0:T(4,128)(2,1)S(1)} %copy.59) | copy-start | bytes 1572868
  134.1 12.1 %copy-start.10 = (f32[1,1024]{1,0:T(1,128)S(1)}, f32[1,1024]{1,0:T(1,128)}, u32[]{:S(2)}) copy-start(f32[1,1024]{1,0:T(1,128)} %param.16) | copy-start | bytes 12292
  141.0 72.4 %all-to-all-start.1 = ((f32[16,64,1024]{2,1,0:T(8,128)}), f32[16,64,1024]{2,1,0:T(8,128)}, u32[]{:S(2)}, u32[]{:S(2)}) async-start(f32[16,64,1024]{2,1,0:T(8,128)} %fusion.47), calls=%async_computation.1 | async-start | bytes 8388608 | tf_op jit(solution)/shard_map/all_to_all | solution.py:34
  216.0 43.7 %collective-permute-start = (bf16[64,1024]{1,0:T(8,128)(2,1)S(1)}, bf16[64,1024]{1,0:T(8,128)(2,1)S(1)}, u32[]{:S(2)}, u32[]{:S(2)}) collective-permute-start(bf16[64,1024]{1,0:T(8,128)(2,1)S(1)} %multiply_convert_fusion), channel_id=1, source_target_pairs={{0,16},{16,32},{32,48},{48,64},{64,80},{80,96},{96,112},{1,17},{17... | collective-permute-start | bytes 393224 | tf_op jit(solution)/shard_map/ppermute | solution.py:41
Sparse Core Ops, SparseCore 0:
  10.1 73.9 all-gather.2
  132.8 115.4 all-gather.4
where the time goes:
time: 276 us; the launch traced here: 275 us
  waiting for transfers between devices  163 us (59%)
  local copies, waits for them, and re-layouts  34.8 us (13%)
  matrix products  26.9 us (10%)
  between operations  20.7 us (8%)
  blocking collectives  11.2 us (4%)
  starting transfers between devices  10.4 us (4%)
  other arithmetic  8.08 us (3%)
    all_gather x1, waiting for transfers between devices, body(): shard_rows = lax.all_gather(wavefunction, 'row', axis=0, tiled=True)  68.5 us
    all_to_all x1, waiting for transfers between devices, sent_and_summed(): lax.all_to_all(parts, axis, split_axis=0, concat_axis=0, tiled=True)  67 us
    all_gather x1, waiting for transfers between devices, body(): shard_rows = lax.all_gather(wave_new, 'row', axis=0, tiled=True)  26.5 us
    reshape x1, local copies, waits for them, and re-layouts, body(): rows_flat = shard_rows.reshape(how_many, 4 * bond_dim)  13.7 us
    all_gather x1, local copies, waits for them, and re-layouts, body(): shard_rows = lax.all_gather(wave_new, 'row', axis=0, tiled=True)  11.4 us
    all_to_all x1, blocking collectives, copy_for_each(): return lax.all_to_all(copies, axis, split_axis=0, concat_axis=0, tiled=True)  11.2 us
    dot_general x1, matrix products, body(): left_z = jnp.dot(left_edge, rows_flat, preferred_element_type=jnp.float32)  6.19 us
    dot_general x1, matrix products, body(): jnp.dot(previous, shard_rows.reshape(how_many, 4 * bond_dim), preferred_e...  6.04 us
  transfers between devices with their start and end apart: 4, of which 3 were waited for; matrix products, arithmetic and copies ran while one was open for 11% of the time, Pallas kernels for 0%

commit v1 on v0

--- a/solution.py
+++ b/solution.py
@@ -102,7 +102,9 @@
     inverse_rows = lax.dynamic_slice_in_dim(inverse, offset, row_count, 0)
     weighted = (inverse_rows[:, None] * gram * inverse[None, :]).astype(jnp.bfloat16)
     previous = passed_along(weighted, "seg", 1)
-    shard_rows = lax.all_gather(wave_new, "row", axis=0, tiled=True)
+    shard_rows = jnp.concatenate(
+        lax.all_to_all(jnp.stack([wave_new] * lax.axis_size("row")), "row", 0, 0), axis=0
+    )
     how_many = shard_rows.shape[0]
     joined = jnp.dot(
         previous, shard_rows.reshape(how_many, 4 * bond_dim), preferred_element_type=jnp.float32

time: 276 us -> 351 us (1.27)
  blocking collectives: 11.2 us -> 64.5 us
  waiting for transfers between devices: 163 us -> 178 us
  local copies, waits for them, and re-layouts: 34.8 us -> 41.2 us
    all_to_all x0 -> x1, blocking collectives: none -> 53.3 us  [sent_and_summed(): lax.all_to_all(parts, axis, split_axis=0, concat_axis=0, tiled=True)]
    all_to_all x1, waiting for transfers between devices: 67 us -> 109 us  [body(): lax.all_to_all(jnp.stack([wave_new] * lax.axis_size('row')), 'row', 0, 0)]
    all_gather x1 -> x0, waiting for transfers between devices: 26.5 us -> none  [body(): shard_rows = lax.all_gather(wave_new, 'row', axis=0, tiled=True)]
    all_gather x1 -> x0, local copies, waits for them, and re-layouts: 11.4 us -> none  [body(): shard_rows = lax.all_gather(wave_new, 'row', axis=0, tiled=True)]
    unnamed x27 -> x28, local copies, waits for them, and re-layouts: 1.52 us -> 12.6 us
    another operation x0 -> x1, local copies, waits for them, and re-layouts: none -> 6.75 us  [body(): jnp.stack([wave_new] * lax.axis_size('row'))]
  transfers between devices with their start and end apart: 4 -> 3, of which waited for: 3 -> 2; matrix products, arithmetic and copies ran while one was open for 11% -> 7% of each run, Pallas kernels for 0% -> 0%
where the time goes in v1:
time: 351 us; the launch traced here: 347 us
  waiting for transfers between devices  178 us (51%)
  blocking collectives  64.5 us (18%)
  local copies, waits for them, and re-layouts  41.2 us (12%)
  matrix products  24 us (7%)
  between operations  20.7 us (6%)
  starting transfers between devices  11.2 us (3%)
  other arithmetic  7.35 us (2%)
    all_to_all x1, waiting for transfers between devices, body(): lax.all_to_all(jnp.stack([wave_new] * lax.axis_size('row')), 'row', 0, 0)  109 us
    all_gather x1, waiting for transfers between devices, body(): shard_rows = lax.all_gather(wavefunction, 'row', axis=0, tiled=True)  68.4 us
    all_to_all x1, blocking collectives, sent_and_summed(): lax.all_to_all(parts, axis, split_axis=0, concat_axis=0, tiled=True)  53.3 us
    reshape x1, local copies, waits for them, and re-layouts, body(): rows_flat = shard_rows.reshape(how_many, 4 * bond_dim)  13.7 us
    unnamed x28, local copies, waits for them, and re-layouts  12.6 us
    all_to_all x1, blocking collectives, copy_for_each(): return lax.all_to_all(copies, axis, split_axis=0, concat_axis=0, tiled=True)  11.2 us
  transfers between devices with their start and end apart: 3, of which 2 were waited for; matrix products, arithmetic and copies ran while one was open for 7% of the time, Pallas kernels for 0%

profile of v1, /device:TPU:1, one launch (start us, length us, event | category | flops | bytes accessed | tf_op | source)
XLA Modules:
  0.0 347.3 jit_solution(4285687756170507353)
XLA Ops:
  7.2 0.0 copy-start
  7.2 0.0 all-gather.2.cloned.1.call-start
  7.2 0.7 all-gather.2.cloned.1.call-update
  7.9 1.4 fusion.46
  9.3 1.2 copy_convert_fusion
  10.5 0.9 fusion.43
  11.4 0.9 fusion.44
  12.3 3.4 fusion.20
  15.7 68.4 %all-gather.2.cloned.1.call-done = bf16[1024,4,1024]{2,1,0:T(4,128)(2,1)} async-done(((bf16[64,4,1024]{2,1,0:T(4,128)(2,1)}), bf16[1024,4,1024]{2,1,0:T(4,128)(2,1)}) %all-gather.2.cloned.1.call-update) | async-done | bytes 8388624 | tf_op jit(solution)/shard_map/all_gather | solution.py:53
  84.1 13.7 %copy.61 = bf16[1024,4,1024]{0,2,1:T(8,128)(2,1)} copy(bf16[1024,4,1024]{2,1,0:T(4,128)(2,1)} %all-gather.2.cloned.1.call-done) | data formatting | bytes 16777216 | tf_op jit(solution)/shard_map/reshape | solution.py:55
  97.9 0.0 copy-done.9
  97.9 0.0 copy-start.2
  97.9 0.0 copy-start.5
  97.9 0.0 copy-start.6
  97.9 0.0 copy-start.12
  97.9 6.2 %fusion.29 = f32[64,4,1024]{2,0,1:T(8,128)S(1)} fusion(bf16[1024,4,1024]{0,2,1:T(8,128)(2,1)} %copy.61, f32[4]{0:T(128)S(1)} %copy-done.11, bf16[64,1024]{1,0:T(8,128)(2,1)S(1)} %copy-done.9), kind=kOutput, calls=%fused_computation.21 | convolution fusion | flops 537133056 | bytes 9568272 | tf_op jit(solution)/shard_map/dot_general | solution.py:57
  104.1 3.6 %fusion.26 = f32[64,4,1024]{2,0,1:T(8,128)S(1)} fusion(f32[64,4,1024]{2,0,1:T(8,128)S(1)} %fusion.29, bf16[1024,4,1024]{0,2,1:T(8,128)(2,1)S(1)} %copy-done.1, bf16[64,1024]{1,0:T(8,128)(2,1)} %param.11), kind=kOutput, calls=%fused_computation.20 | convolution fusion | flops 537133056 | bytes 10616832 | tf_op jit(solution)/shard_map/dot_general | solution.py:56
  107.7 0.0 copy-done
  107.7 0.0 copy-done.2
  107.7 0.0 copy-done.4
  107.7 0.0 copy-done.5
  107.7 0.0 copy-done.6
  107.8 0.0 copy-done.7
  107.8 0.0 copy-done.8
  107.8 0.0 copy-done.12
  107.8 4.2 %fusion.33 = (f32[]{:T(128)}, f32[]{:T(128)}, f32[]{:T(128)}, f32[64,4,1024]{2,0,1:T(8,128)}) fusion(bf16[64,4,1024]{2,1,0:T(4,128)(2,1)S(1)} %copy-done.2, f32[64,1,1024]{2,0,1:T(8,128)S(1)} %copy-done.8, f32[64,1,1024]{2,0,1:T(8,128)S(1)} %copy-done.6, f32[64,1,1024]{2,0,1:T(8,128)S(1)} %copy-done.7, f32[64,1,1024]{2,0,1:T(8,128)S(1)} %get-tuple-element.26, ...), kind=kOutput, calls=%fused_computation.23 | convolution fusion | flops 541851648 | bytes 7864356 | tf_op jit(solution)/shard_map/dot_general | solution.py:61
  112.0 2.0 pad_maximum_fusion
  114.0 11.2 %all_to_all.16 = f32[16,1,3]{2,1,0:T(1,128)S(1)} all-to-all(f32[16,1,3]{2,1,0:T(1,128)S(1)} %broadcast_in_dim.11), channel_id=1, replica_groups=mesh['seg'=8,'row'=16] {'row'}, dimensions={0} | all-to-all | bytes 384 | tf_op jit(solution)/shard_map/all_to_all | solution.py:11
  125.3 0.6 fusion.45
  130.5 1.5 fusion.37
  132.1 0.4 copy.60
  132.5 0.0 copy-start.3
  132.5 0.1 reshape.89
  132.6 0.9 reshape.82
  133.5 2.0 copy.58
  135.6 1.7 fusion.47
  137.3 53.3 %all_to_all.17 = f32[16,64,1024]{2,1,0:T(8,128)} all-to-all(f32[16,64,1024]{2,1,0:T(8,128)S(1)} %fusion.47), channel_id=1, replica_groups=mesh['seg'=8,'row'=16] {'row'}, dimensions={0} | all-to-all | bytes 8388608 | tf_op jit(solution)/shard_map/all_to_all | solution.py:34
  190.6 6.7 %stack.5 = bf16[16,64,4,1024]{3,2,1,0:T(4,128)(2,1)} broadcast(bf16[64,4,1024]{2,1,0:T(4,128)(2,1)S(1)} %copy.60), dimensions={1,2,3} | broadcast | bytes 8912896 | tf_op jit(solution)/shard_map/stack | solution.py:106
  197.3 5.1 %all-to-all-start.2 = ((bf16[16,64,4,1024]{3,2,1,0:T(4,128)(2,1)}), bf16[16,64,4,1024]{3,2,1,0:T(4,128)(2,1)}, u32[]{:S(2)}, u32[]{:S(2)}) async-start(bf16[16,64,4,1024]{3,2,1,0:T(4,128)(2,1)} %stack.5), calls=%async_computation.2 | async-start | bytes 16777216 | tf_op jit(solution)/shard_map/all_to_all | solution.py:106
  203.1 0.1 dynamic_slice.3
  203.2 2.5 reduce_sum.49
  205.7 0.1 multiply_convert_fusion
  205.8 6.1 %collective-permute-start = (bf16[64,1024]{1,0:T(8,128)(2,1)S(1)}, bf16[64,1024]{1,0:T(8,128)(2,1)S(1)}, u32[]{:S(2)}, u32[]{:S(2)}) collective-permute-start(bf16[64,1024]{1,0:T(8,128)(2,1)S(1)} %multiply_convert_fusion), channel_id=1, source_target_pairs={{0,16},{16,32},{32,48},{48,64},{64,80},{80,96},{96,112},{1,17},{17... | collective-permute-start | bytes 393224 | tf_op jit(solution)/shard_map/ppermute | solution.py:41
  211.9 109.2 %all-to-all-done.2 = bf16[16,64,4,1024]{3,2,1,0:T(4,128)(2,1)} async-done(((bf16[16,64,4,1024]{3,2,1,0:T(4,128)(2,1)}), bf16[16,64,4,1024]{3,2,1,0:T(4,128)(2,1)}, u32[]{:S(2)}, u32[]{:S(2)}) %all-to-all-start.2) | async-done | bytes 8388640 | tf_op jit(solution)/shard_map/all_to_all | solution.py:106
  321.1 12.1 %copy.66 = bf16[128,8,4,1024]{3,1,2,0:T(8,128)(2,1)} copy(bf16[128,8,4,1024]{3,2,1,0:T(4,128)(2,1)} %bitcast.24) | data formatting | bytes 16777216
  333.2 0.0 collective-permute-done
  333.2 4.9 %convolution_convert_fusion = bf16[64,4096]{1,0:T(8,128)(2,1)S(1)} fusion(bf16[64,1024]{1,0:T(8,128)(2,1)S(1)} %collective-permute-done, bf16[1024,4096]{1,0:T(8,128)(2,1)} %bitcast.62), kind=kOutput, calls=%fused_computation.4 | convolution fusion | flops 537133056 | bytes 9043968 | tf_op jit(solution)/shard_map/dot_general | solution.py:109
  338.2 1.2 reshape.83
  (15 shorter events, 0.1 us)
Async XLA Ops:
  7.2 100.5 %copy-start = (bf16[1024,1024]{1,0:T(8,128)(2,1)S(1)}, bf16[1024,1024]{1,0:T(8,128)(2,1)}, u32[]{:S(2)}) copy-start(bf16[1024,1024]{1,0:T(8,128)(2,1)} %param.13) | copy-start | bytes 6291460
  7.2 77.0 %all-gather.2.cloned.1.call-start = ((), (), s32[]{:S(2)}) async-start(), calls=%async_computation.3 | async-start | bytes 8912896 | tf_op jit(solution)/shard_map/all_gather | solution.py:53
  15.7 82.1 %copy-start.9 = (bf16[64,1024]{1,0:T(8,128)(2,1)S(1)}, bf16[64,1024]{1,0:T(8,128)(2,1)}, u32[]{:S(2)}) copy-start(bf16[64,1024]{1,0:T(8,128)(2,1)} %param.12) | copy-start | bytes 393220
  15.7 82.2 %copy-start.11 = (f32[4]{0:T(128)S(1)}, f32[4]{0:T(128)}, u32[]{:S(2)}) copy-start(f32[4]{0:T(128)} %constant.24.clone) | copy-start | bytes 52
  97.9 6.3 %copy-start.1 = (bf16[1024,4,1024]{0,2,1:T(8,128)(2,1)S(1)}, bf16[1024,4,1024]{0,2,1:T(8,128)(2,1)}, u32[]{:S(2)}) copy-start(bf16[1024,4,1024]{0,2,1:T(8,128)(2,1)} %copy.61) | copy-start | bytes 25165828
  97.9 9.9 %copy-start.2 = (bf16[64,4,1024]{2,1,0:T(4,128)(2,1)S(1)}, bf16[64,4,1024]{2,1,0:T(4,128)(2,1)}, u32[]{:S(2)}) copy-start(bf16[64,4,1024]{2,1,0:T(4,128)(2,1)} %param.10) | copy-start | bytes 1572868
  97.9 9.8 %copy-start.4 = (f32[64,4,1024]{2,0,1:T(8,128)S(1)}, f32[64,4,1024]{2,0,1:T(8,128)}, u32[]{:S(2)}) copy-start(f32[64,4,1024]{2,0,1:T(8,128)} %fusion.20) | copy-start | bytes 3145732
  97.9 9.8 %copy-start.5 = (f32[64,2,1024]{2,0,1:T(8,128)S(1)}, f32[64,2,1024]{2,0,1:T(8,128)}, u32[]{:S(2)}) copy-start(f32[64,2,1024]{2,0,1:T(8,128)} %get-tuple-element.31) | copy-start | bytes 1572868
  97.9 9.8 %copy-start.6 = (f32[64,1,1024]{2,0,1:T(8,128)S(1)}, f32[64,1,1024]{2,0,1:T(8,128)}, u32[]{:S(2)}) copy-start(f32[64,1,1024]{2,0,1:T(8,128)} %get-tuple-element.27) | copy-start | bytes 786436
  97.9 9.8 %copy-start.7 = (f32[64,1,1024]{2,0,1:T(8,128)S(1)}, f32[64,1,1024]{2,0,1:T(8,128)}, u32[]{:S(2)}) copy-start(f32[64,1,1024]{2,0,1:T(8,128)} %get-tuple-element.28) | copy-start | bytes 786436
  97.9 9.8 %copy-start.8 = (f32[64,1,1024]{2,0,1:T(8,128)S(1)}, f32[64,1,1024]{2,0,1:T(8,128)}, u32[]{:S(2)}) copy-start(f32[64,1,1024]{2,0,1:T(8,128)} %get-tuple-element.29) | copy-start | bytes 786436
  97.9 9.8 %copy-start.12 = (f32[4]{0:T(128)S(1)}, f32[4]{0:T(128)}, u32[]{:S(2)}) copy-start(f32[4]{0:T(128)} %constant.32) | copy-start | bytes 52
  132.5 58.1 %copy-start.3 = (bf16[64,4,1024]{2,1,0:T(4,128)(2,1)}, bf16[64,4,1024]{2,1,0:T(4,128)(2,1)S(1)}, u32[]{:S(2)}) copy-start(bf16[64,4,1024]{2,1,0:T(4,128)(2,1)S(1)} %copy.60) | copy-start | bytes 1572868
  197.3 5.7 %copy-start.10 = (f32[1,1024]{1,0:T(1,128)S(1)}, f32[1,1024]{1,0:T(1,128)}, u32[]{:S(2)}) copy-start(f32[1,1024]{1,0:T(1,128)} %param.16) | copy-start | bytes 12292
  197.3 123.7 %all-to-all-start.2 = ((bf16[16,64,4,1024]{3,2,1,0:T(4,128)(2,1)}), bf16[16,64,4,1024]{3,2,1,0:T(4,128)(2,1)}, u32[]{:S(2)}, u32[]{:S(2)}) async-start(bf16[16,64,4,1024]{3,2,1,0:T(4,128)(2,1)} %stack.5), calls=%async_computation.2 | async-start | bytes 16777216 | tf_op jit(solution)/shard_map/all_to_all | solution.py:106
  205.8 127.4 %collective-permute-start = (bf16[64,1024]{1,0:T(8,128)(2,1)S(1)}, bf16[64,1024]{1,0:T(8,128)(2,1)S(1)}, u32[]{:S(2)}, u32[]{:S(2)}) collective-permute-start(bf16[64,1024]{1,0:T(8,128)(2,1)S(1)} %multiply_convert_fusion), channel_id=1, source_target_pairs={{0,16},{16,32},{32,48},{48,64},{64,80},{80,96},{96,112},{1,17},{17... | collective-permute-start | bytes 393224 | tf_op jit(solution)/shard_map/ppermute | solution.py:41
Sparse Core Ops, SparseCore 0:
  10.1 73.9 all-gather.1
